TPU v7x, 256 devices: a whole 4x4x8 slice. The times are simulated.
256 devices in a mesh: gx: 16 (over z_lo, x, core), gy: 4 (over y), tx: 4 (over z_hi).
Axes of the slice: x: 4, y: 4, z: 8 (z_hi: 4, z_lo: 2; z = z_hi * 2 + z_lo), core: 2. Of those that a mesh axis runs over, the one named last changes fastest.
Arguments:
- src_cell: int32 [8], P('tx'), may hold values from 0 to 524287
- basis: bfloat16 [16, 2, 3, 8, 128, 512], P('tx', None, None, None, 'gx', 'gy'), as said below
- images: bfloat16 [16, 2, 3, 8, 128, 512], P('tx', None, None, None, 'gx', 'gy'), as said below
- induction: bfloat16 [3, 8, 128, 512], P(None, 'tx', 'gx', 'gy'), may hold values from 0.25 to 4
Outputs:
- solution: float32 [8, 2, 3, 8, 128, 512], P('tx', None, None, None, 'gx', 'gy')
- residual: float32 [8, 2, 3, 8, 128, 512], P('tx', None, None, None, 'gx', 'gy')
Inputs may be any that keep to these rules, and one draw needn't show every extreme that they name: `basis`: entries of order one. `images`: entries of order one.
All inputs are finite; a program needn't handle non-finite values.
Results may differ from a plain program's by a relative error of at most 0.0003.
Values may be sent and summed in bfloat16 or wider, within the bound.
No kernel may reach another device: no remote copies, remote signals or barrier semaphores. Data moves between devices by JAX's collectives and lax.ppermute only.
A program may use at most 64 MiB of HBM per device.

v0:
```python
import jax
import jax.numpy as jnp
from jax import lax
from jax.sharding import PartitionSpec as P

CYCLES = 2
ARNOLDI = 2
eps = 1e-06


def with_halo(x, sides, width):
    for axis, dim in sides:
        size, length = (lax.axis_size(axis), x.shape[dim])
        up = [(i, (i + 1) % size) for i in range(size - 1)]
        down = [(j, i) for i, j in up]
        last = lax.slice_in_dim(x, length - width, length, axis=dim)
        initial = lax.slice_in_dim(x, 0, width, axis=dim)
        before = lax.ppermute(last, axis, up)
        after = lax.ppermute(initial, axis, down)
        x = jnp.concatenate([before, x, after], axis=dim)
    return x


def differ(field, axis, forward):
    axis = field.ndim + axis
    count = field.shape[axis]
    delta = lax.slice_in_dim(field, 1, count, axis=axis) - lax.slice_in_dim(
        field, 0, count - 1, axis=axis
    )
    zero = jnp.zeros_like(lax.slice_in_dim(field, 0, 1, axis=axis))
    if forward:
        return jnp.concatenate([delta, zero], axis=axis)
    return jnp.concatenate([zero, delta], axis=axis)


def curl_curl(padded):
    e_x = padded[..., 0, :, :, :]
    e_y = padded[..., 1, :, :, :]
    e_z = padded[..., 2, :, :, :]
    b_x = differ(e_z, -1, True) - differ(e_y, -3, True)
    b_y = differ(e_x, -3, True) - differ(e_z, -2, True)
    b_z = differ(e_y, -2, True) - differ(e_x, -1, True)
    c_x = differ(b_z, -1, False) - differ(b_y, -3, False)
    c_y = differ(b_x, -3, False) - differ(b_z, -2, False)
    c_z = differ(b_y, -2, False) - differ(b_x, -1, False)
    whole = jnp.stack([c_x, c_y, c_z], axis=-4)
    return whole[..., 1:-1, 1:-1, 1:-1]


def apply_operator(field, induct):
    framed = with_halo(field, (("gx", 4), ("gy", 5)), 1)
    padded = jnp.pad(framed, [(0, 0), (0, 0), (0, 0), (1, 1), (0, 0), (0, 0)])
    curled = curl_curl(padded)
    real_part = curled[:, 0] - induct[None] * field[:, 1]
    imag_part = curled[:, 1] + induct[None] * field[:, 0]
    return jnp.stack([real_part, imag_part], axis=1)


def source_field(cells, z_pos, x_pos, y_pos, size_x, size_y, induct):
    plane = size_x * size_y
    src_z = cells // plane
    rest = cells % plane
    src_x = rest // size_y
    src_y = rest % size_y
    d_z = (z_pos[None, :] - src_z[:, None]).astype(jnp.float32)
    d_x = (x_pos[None, :] - src_x[:, None]).astype(jnp.float32)
    d_y = (y_pos[None, :] - src_y[:, None]).astype(jnp.float32)
    dist = jnp.sqrt(
        d_z[:, :, None, None] ** 2 + d_x[:, None, :, None] ** 2 + d_y[:, None, None, :] ** 2
    )
    primary = jnp.exp(-dist / ((size_x + size_y) / 8.0))
    weights = jnp.array([1.0, 0.5, 0.25], dtype=jnp.float32)
    real_part = (induct - 1.0)[None] * weights[None, :, None, None, None] * primary[:, None]
    return jnp.stack([real_part, 0.5 * real_part], axis=1)


def inner_basis(vectors, field):
    return jnp.einsum(
        "kpczxy,spczxy->ks",
        vectors,
        field,
        precision=lax.Precision.HIGHEST,
        preferred_element_type=jnp.float32,
    )


def combine(coeffs, vectors):
    return jnp.einsum(
        "ks,kpczxy->spczxy",
        coeffs,
        vectors,
        precision=lax.Precision.HIGHEST,
        preferred_element_type=jnp.float32,
    )


def per_source(left, right):
    return jnp.sum(left * right, axis=(1, 2, 3, 4, 5))


def expand(values):
    return values[:, None, None, None, None, None]


def small_solve(matrix, rhs):
    factor = jnp.linalg.cholesky(matrix)
    return jax.scipy.linalg.cho_solve((factor, True), rhs)


def on_device(src_cell, basis, images, induction):
    all_basis, all_images, gathered = (
        lax.all_gather(basis, "tx", axis=0, tiled=True),
        lax.all_gather(images, "tx", axis=0, tiled=True),
        lax.all_gather(induction, "tx", axis=1, tiled=True),
    )
    induct = gathered.astype(jnp.float32)
    depth = basis.shape[3]
    width_x = basis.shape[4]
    width_y = basis.shape[5]
    size_x = width_x * lax.axis_size("gx")
    size_y = width_y * lax.axis_size("gy")
    z_pos = jnp.arange(depth, dtype=jnp.int32)
    x_pos = lax.axis_index("gx") * width_x + jnp.arange(width_x, dtype=jnp.int32)
    y_pos = lax.axis_index("gy") * width_y + jnp.arange(width_y, dtype=jnp.int32)
    rhs = source_field(src_cell, z_pos, x_pos, y_pos, size_x, size_y, induct)
    gram_part = jnp.einsum(
        "kpczxy,lpczxy->kl", all_images, all_images, preferred_element_type=jnp.float32
    )
    gram, start_inner = lax.psum((gram_part, inner_basis(all_images, rhs)), ("gx", "gy"))
    factor = jnp.linalg.cholesky(gram)
    h_zero = jax.scipy.linalg.cho_solve((factor, True), start_inner)
    residual = rhs - combine(h_zero, all_images)
    solution = combine(h_zero, all_basis)
    for cycle in range(CYCLES):
        beta = jnp.sqrt(lax.psum(per_source(residual, residual), ("gx", "gy")) + eps)
        krylov = [residual / expand(beta)]
        h_cols = []
        g_cols = []
        for step in range(ARNOLDI):
            work = apply_operator(krylov[step], induct)
            g_raw = lax.psum(inner_basis(all_images, work), ("gx", "gy"))
            g_now = jax.scipy.linalg.cho_solve((factor, True), g_raw)
            work = work - combine(g_now, all_images)
            h_now = lax.psum(jnp.stack([per_source(vec, work) for vec in krylov]), ("gx", "gy"))
            for index in range(step + 1):
                work = work - expand(h_now[index]) * krylov[index]
            h_next = jnp.sqrt(lax.psum(per_source(work, work), ("gx", "gy")) + eps)
            krylov.append(work / expand(h_next))
            pad_rows = jnp.zeros((ARNOLDI - step - 1, h_next.shape[0]), dtype=jnp.float32)
            h_cols.append(jnp.concatenate([h_now, h_next[None], pad_rows], axis=0))
            g_cols.append(g_now)
        hess = jnp.stack(h_cols, axis=1)
        g_all = jnp.stack(g_cols, axis=1)
        normal = jnp.einsum("ijs,iks->sjk", hess, hess, precision=lax.Precision.HIGHEST)
        target = beta[:, None] * jnp.transpose(hess[0])
        y_coef = jax.vmap(small_solve)(normal, target)
        update = expand(y_coef[:, 0]) * krylov[0]
        step = 1
        update = update + expand(y_coef[:, step]) * krylov[step]
        u_coef = jnp.einsum("kjs,sj->ks", g_all, y_coef, precision=lax.Precision.HIGHEST)
        solution = solution + update - combine(u_coef, all_basis)
        first = jnp.zeros((ARNOLDI + 1, beta.shape[0]), dtype=jnp.float32).at[0].set(beta)
        t_coef = first - jnp.einsum("ijs,sj->is", hess, y_coef, precision=lax.Precision.HIGHEST)
        residual = expand(t_coef[0]) * krylov[0]
        for index in range(1, ARNOLDI + 1):
            residual = residual + expand(t_coef[index]) * krylov[index]
    return (solution, residual)


def solution(mesh):
    in_specs = (
        P("tx"),
        P("tx", None, None, None, "gx", "gy"),
        P("tx", None, None, None, "gx", "gy"),
        P(None, "tx", "gx", "gy"),
    )
    out_specs = (P("tx", None, None, None, "gx", "gy"), P("tx", None, None, None, "gx", "gy"))
    return jax.shard_map(
        on_device, mesh=mesh, in_specs=in_specs, out_specs=out_specs, check_vma=False
    )
```

profile of v0, /device:TPU:40, one launch (start us, length us, event | category | flops | bytes accessed | tf_op | source)
XLA Modules:
  0.0 2366.0 jit_solution(5453150176349590648)
XLA Ops:
  7.9 16.6 all_gather.10
  26.5 26.6 %all-gather.3.cloned.1.call-done = bf16[16,2,3,8,8,128]{5,4,3,2,1,0:T(8,128)(2,1)} async-done(((bf16[4,2,3,8,8,128]{5,4,3,2,1,0:T(8,128)(2,1)}), bf16[16,2,3,8,8,128]{5,4,3,2,1,0:T(8,128)(2,1)}) %all-gather.3.cloned.1.call-update) | async-done | bytes 1572880 | tf_op jit(solution)/shard_map/all_gather | solution.py:113
  53.1 5.4 convolution_bitcast_fusion
  58.5 3.7 convolution_bitcast_fusion.8
  62.2 144.3 %all-reduce.54 = (f32[16,2]{0,1:T(2,128)S(1)}, f32[16,16]{0,1:T(8,128)S(1)}) all-reduce(f32[16,2]{0,1:T(2,128)S(1)} %convolution_bitcast_fusion.8, f32[16,16]{0,1:T(8,128)S(1)} %convolution_bitcast_fusion), channel_id=1, replica_groups=mesh['gx'=16,'gy'=4,'tx'=4] {'gx','gy'}, use_global_device_ids=true, to_apply=%region_3.4 | all-reduce | flops 288 | bytes 2304 | tf_op jit(solution)/shard_map/psum | solution.py:129
  206.6 1.5 cholesky.32
  210.9 3.3 multiply_reduce_fusion.11
  214.2 143.8 %psum.114 = f32[2]{0:T(128)S(1)} all-reduce(f32[2]{0:T(128)S(1)} %get-tuple-element.119), channel_id=1, replica_groups=mesh['gx'=16,'gy'=4,'tx'=4] {'gx','gy'}, use_global_device_ids=true, to_apply=%region_5.7 | all-reduce | flops 2 | bytes 16 | tf_op jit(solution)/shard_map/psum | solution.py:135
  358.2 1.9 collective-permute-start
  360.2 5.8 collective-permute-start.1
  366.0 1.7 collective-permute-done.1
  368.5 1.9 collective-permute-start.2
  370.4 4.1 collective-permute-start.3
  374.6 4.7 collective-permute-done.2
  379.3 1.9 collective-permute-done.3
  381.2 2.4 select_maximum_fusion.12
  391.2 3.7 convolution_bitcast_fusion.7
  394.9 140.9 %psum.115 = f32[16,2]{0,1:T(2,128)S(1)} all-reduce(f32[16,2]{0,1:T(2,128)S(1)} %convolution_bitcast_fusion.7), channel_id=1, replica_groups=mesh['gx'=16,'gy'=4,'tx'=4] {'gx','gy'}, use_global_device_ids=true, to_apply=%region_6.8 | all-reduce | flops 32 | bytes 256 | tf_op jit(solution)/shard_map/psum | solution.py:141
  536.1 3.3 multiply_reduce_fusion.10
  539.4 139.6 %psum.116 = f32[1,2]{1,0:T(1,128)S(1)} all-reduce(f32[1,2]{1,0:T(1,128)S(1)} %bitcast.337), channel_id=1, replica_groups=mesh['gx'=16,'gy'=4,'tx'=4] {'gx','gy'}, use_global_device_ids=true, to_apply=%region_8.10 | all-reduce | flops 2 | bytes 16 | tf_op jit(solution)/shard_map/psum | solution.py:144
  679.7 139.5 %psum.117 = f32[2]{0:T(128)S(1)} all-reduce(f32[2]{0:T(128)S(1)} %get-tuple-element.49), channel_id=1, replica_groups=mesh['gx'=16,'gy'=4,'tx'=4] {'gx','gy'}, use_global_device_ids=true, to_apply=%region_10.12 | all-reduce | flops 2 | bytes 16 | tf_op jit(solution)/shard_map/psum | solution.py:147
  819.5 1.9 collective-permute-start.4
  821.4 5.8 collective-permute-start.5
  827.2 1.6 collective-permute-done.5
  829.7 1.9 collective-permute-start.6
  831.6 3.9 collective-permute-start.7
  835.6 4.9 collective-permute-done.6
  840.5 1.9 collective-permute-done.7
  842.4 2.4 select_maximum_fusion.8
  852.5 3.6 convolution_bitcast_fusion.6
  856.1 141.1 %psum.118 = f32[16,2]{0,1:T(2,128)S(1)} all-reduce(f32[16,2]{0,1:T(2,128)S(1)} %convolution_bitcast_fusion.6), channel_id=1, replica_groups=mesh['gx'=16,'gy'=4,'tx'=4] {'gx','gy'}, use_global_device_ids=true, to_apply=%region_11.13 | all-reduce | flops 32 | bytes 256 | tf_op jit(solution)/shard_map/psum | solution.py:141
  997.4 3.4 multiply_reduce_fusion.8
  1000.9 139.0 %psum.119 = f32[2,2]{1,0:T(2,128)S(1)} all-reduce(f32[2,2]{1,0:T(2,128)S(1)} %pad_maximum_fusion.26), channel_id=1, replica_groups=mesh['gx'=16,'gy'=4,'tx'=4] {'gx','gy'}, use_global_device_ids=true, to_apply=%region_14.16 | all-reduce | flops 4 | bytes 32 | tf_op jit(solution)/shard_map/psum | solution.py:144
  1140.6 140.2 %psum.120 = f32[2]{0:T(128)S(1)} all-reduce(f32[2]{0:T(128)S(1)} %get-tuple-element.47), channel_id=1, replica_groups=mesh['gx'=16,'gy'=4,'tx'=4] {'gx','gy'}, use_global_device_ids=true, to_apply=%region_16.18 | all-reduce | flops 2 | bytes 16 | tf_op jit(solution)/shard_map/psum | solution.py:147
  1283.8 139.0 %psum.121 = f32[2]{0:T(128)S(1)} all-reduce(f32[2]{0:T(128)S(1)} %get-tuple-element.45), channel_id=1, replica_groups=mesh['gx'=16,'gy'=4,'tx'=4] {'gx','gy'}, use_global_device_ids=true, to_apply=%region_20.24 | all-reduce | flops 2 | bytes 16 | tf_op jit(solution)/shard_map/psum | solution.py:135
  1423.1 1.9 collective-permute-start.8
  1425.0 5.8 collective-permute-start.9
  1430.8 3.7 convolution_add_fusion
  1435.4 1.9 collective-permute-start.10
  1437.3 4.1 collective-permute-start.11
  1441.5 5.5 collective-permute-done.10
  1447.1 1.9 collective-permute-done.11
  1449.0 2.4 select_maximum_fusion.4
  1459.0 3.7 convolution_bitcast_fusion.5
  1462.7 140.7 %psum.122 = f32[16,2]{0,1:T(2,128)S(1)} all-reduce(f32[16,2]{0,1:T(2,128)S(1)} %convolution_bitcast_fusion.5), channel_id=1, replica_groups=mesh['gx'=16,'gy'=4,'tx'=4] {'gx','gy'}, use_global_device_ids=true, to_apply=%region_21.25 | all-reduce | flops 32 | bytes 256 | tf_op jit(solution)/shard_map/psum | solution.py:141
  1603.7 3.3 multiply_reduce_fusion.4
  1607.0 138.7 %psum.123 = f32[1,2]{1,0:T(1,128)S(1)} all-reduce(f32[1,2]{1,0:T(1,128)S(1)} %bitcast.338), channel_id=1, replica_groups=mesh['gx'=16,'gy'=4,'tx'=4] {'gx','gy'}, use_global_device_ids=true, to_apply=%region_23.27 | all-reduce | flops 2 | bytes 16 | tf_op jit(solution)/shard_map/psum | solution.py:144
  1746.3 140.5 %psum.124 = f32[2]{0:T(128)S(1)} all-reduce(f32[2]{0:T(128)S(1)} %get-tuple-element.43), channel_id=1, replica_groups=mesh['gx'=16,'gy'=4,'tx'=4] {'gx','gy'}, use_global_device_ids=true, to_apply=%region_25.29 | all-reduce | flops 2 | bytes 16 | tf_op jit(solution)/shard_map/psum | solution.py:147
  1887.0 1.9 collective-permute-start.12
  1889.0 5.8 collective-permute-start.13
  1894.9 1.6 collective-permute-done.13
  1897.3 1.9 collective-permute-start.14
  1899.2 3.9 collective-permute-start.15
  1903.2 4.9 collective-permute-done.14
  1908.1 1.9 collective-permute-done.15
  1910.0 2.4 select_maximum_fusion
  1920.0 3.7 convolution_bitcast_fusion.4
  1923.7 140.9 %psum.125 = f32[16,2]{0,1:T(2,128)S(1)} all-reduce(f32[16,2]{0,1:T(2,128)S(1)} %convolution_bitcast_fusion.4), channel_id=1, replica_groups=mesh['gx'=16,'gy'=4,'tx'=4] {'gx','gy'}, use_global_device_ids=true, to_apply=%region_26.30 | all-reduce | flops 32 | bytes 256 | tf_op jit(solution)/shard_map/psum | solution.py:141
  2064.9 3.4 multiply_reduce_fusion.2
  2068.3 139.0 %psum.126 = f32[2,2]{1,0:T(2,128)S(1)} all-reduce(f32[2,2]{1,0:T(2,128)S(1)} %pad_maximum_fusion.27), channel_id=1, replica_groups=mesh['gx'=16,'gy'=4,'tx'=4] {'gx','gy'}, use_global_device_ids=true, to_apply=%region_29.33 | all-reduce | flops 4 | bytes 32 | tf_op jit(solution)/shard_map/psum | solution.py:144
  2208.7 140.2 %psum.127 = f32[2]{0:T(128)S(1)} all-reduce(f32[2]{0:T(128)S(1)} %get-tuple-element.41), channel_id=1, replica_groups=mesh['gx'=16,'gy'=4,'tx'=4] {'gx','gy'}, use_global_device_ids=true, to_apply=%region_31.35 | all-reduce | flops 2 | bytes 16 | tf_op jit(solution)/shard_map/psum | solution.py:147
  2351.1 1.5 multiply_add_fusion
  2353.7 2.7 fusion
  2356.3 1.5 convolution_subtract_fusion
  (209 shorter events, 52.0 us)
Async XLA Ops:
  7.2 46.0 %all-gather.3.cloned.1.call-start = ((), (), s32[]{:S(2)}) async-start(), calls=%async_computation | async-start | bytes 1966080 | tf_op jit(solution)/shard_map/all_gather | solution.py:113
  7.9 1422.9 %all-gather.5.cloned.1.call-start = ((), (), s32[]{:S(2)}) async-start(), calls=%async_computation.1 | async-start | bytes 1966080 | tf_op jit(solution)/shard_map/all_gather | solution.py:112
  53.1 5.4 copy-start.1
  358.2 7.7 collective-permute-start
  360.2 7.5 collective-permute-start.1
  368.5 10.8 collective-permute-start.2
  370.4 10.8 collective-permute-start.3
  389.8 1.4 copy-start.2
  819.5 7.8 collective-permute-start.4
  821.4 7.5 collective-permute-start.5
  829.7 10.8 collective-permute-start.6
  831.6 10.8 collective-permute-start.7
  851.0 1.4 copy-start.3
  1423.1 11.5 collective-permute-start.8
  1425.0 9.5 collective-permute-start.9
  1435.4 11.7 collective-permute-start.10
  1437.3 11.7 collective-permute-start.11
  1457.6 1.4 copy-start.4
  1887.0 7.8 collective-permute-start.12
  1889.0 7.5 collective-permute-start.13
  1897.3 10.8 collective-permute-start.14
  1899.2 10.8 collective-permute-start.15
  1918.6 1.4 copy-start.5
  2349.7 4.0 copy-start
Sparse Core Ops, SparseCore 0:
  9.8 43.2 all-gather.2
  366.1 35.2 all-gather.4
where the time goes:
time: 2380 us; the launch traced here: 2370 us
  blocking collectives  2120 us (89%)
  waiting for transfers between devices  59.9 us (3%)
  starting transfers between devices  54.6 us (2%)
  matrix products  50.6 us (2%)
  other arithmetic  50.3 us (2%)
    psum x4, blocking collectives, on_device(): g_raw = lax.psum(inner_basis(all_images, work), ('gx', 'gy'))  564 us
    psum x4, blocking collectives, on_device(): h_next = jnp.sqrt(lax.psum(per_source(work, work), ('gx', 'gy')) + eps)  560 us
    psum x4, blocking collectives, on_device(): lax.psum(jnp.stack([per_source(vec, work) for vec in krylov]), ('gx', 'gy'))  556 us
    psum x2, blocking collectives, on_device(): lax.psum(per_source(residual, residual), ('gx', 'gy')) + eps  283 us
    psum x1, blocking collectives, on_device(): lax.psum((gram_part, inner_basis(all_images, rhs)), ('gx', 'gy'))  144 us
  transfers between devices with their start and end apart: 18, of which 12 were waited for; matrix products, arithmetic and copies ran while one was open for 2% of the time, Pallas kernels for 0%

commit v1 on v0

--- a/solution.py
+++ b/solution.py
@@ -138,7 +138,7 @@
         g_cols = []
         for step in range(ARNOLDI):
             work = apply_operator(krylov[step], induct)
-            g_raw = lax.psum(inner_basis(all_images, work), ("gx", "gy"))
+            g_raw = jnp.sum(lax.all_gather(inner_basis(all_images, work), ("gx", "gy")), axis=0)
             g_now = jax.scipy.linalg.cho_solve((factor, True), g_raw)
             work = work - combine(g_now, all_images)
             h_now = lax.psum(jnp.stack([per_source(vec, work) for vec in krylov]), ("gx", "gy"))

time: 2380 us -> 2370 us (level)
    psum x4 -> x0, blocking collectives: 564 us -> none  [on_device(): g_raw = lax.psum(inner_basis(all_images, work), ('gx', 'gy'))]
    all_gather x0 -> x4, blocking collectives: none -> 554 us  [on_device(): lax.all_gather(inner_basis(all_images, work), ('gx', 'gy'))]
where the time goes in v1:
time: 2370 us; the launch traced here: 2360 us
  blocking collectives  2110 us (89%)
  waiting for transfers between devices  59.9 us (3%)
  starting transfers between devices  54.6 us (2%)
  other arithmetic  50.6 us (2%)
  matrix products  50.6 us (2%)
    psum x4, blocking collectives, on_device(): h_next = jnp.sqrt(lax.psum(per_source(work, work), ('gx', 'gy')) + eps)  561 us
    psum x4, blocking collectives, on_device(): lax.psum(jnp.stack([per_source(vec, work) for vec in krylov]), ('gx', 'gy'))  556 us
    all_gather x4, blocking collectives, on_device(): lax.all_gather(inner_basis(all_images, work), ('gx', 'gy'))  554 us
    psum x2, blocking collectives, on_device(): lax.psum(per_source(residual, residual), ('gx', 'gy')) + eps  283 us
    psum x1, blocking collectives, on_device(): lax.psum((gram_part, inner_basis(all_images, rhs)), ('gx', 'gy'))  144 us
  transfers between devices with their start and end apart: 18, of which 12 were waited for; matrix products, arithmetic and copies ran while one was open for 2% of the time, Pallas kernels for 0%

profile of v1, /device:TPU:40, one launch (start us, length us, event | category | flops | bytes accessed | tf_op | source)
XLA Modules:
  0.0 2356.7 jit_solution(5946858598461464505)
XLA Ops:
  7.9 16.6 all_gather.34
  26.5 26.6 %all-gather.11.cloned.1.call-done = bf16[16,2,3,8,8,128]{5,4,3,2,1,0:T(8,128)(2,1)} async-done(((bf16[4,2,3,8,8,128]{5,4,3,2,1,0:T(8,128)(2,1)}), bf16[16,2,3,8,8,128]{5,4,3,2,1,0:T(8,128)(2,1)}) %all-gather.11.cloned.1.call-update) | async-done | bytes 1572880 | tf_op jit(solution)/shard_map/all_gather | solution.py:113
  53.1 5.4 convolution_bitcast_fusion
  58.5 3.7 convolution_bitcast_fusion.8
  62.2 144.3 %all-reduce.54 = (f32[16,2]{0,1:T(2,128)S(1)}, f32[16,16]{0,1:T(8,128)S(1)}) all-reduce(f32[16,2]{0,1:T(2,128)S(1)} %convolution_bitcast_fusion.8, f32[16,16]{0,1:T(8,128)S(1)} %convolution_bitcast_fusion), channel_id=1, replica_groups=mesh['gx'=16,'gy'=4,'tx'=4] {'gx','gy'}, use_global_device_ids=true, to_apply=%region_3.4 | all-reduce | flops 288 | bytes 2304 | tf_op jit(solution)/shard_map/psum | solution.py:129
  206.6 1.5 cholesky.32
  210.9 3.3 multiply_reduce_fusion.11
  214.2 143.8 %psum.86 = f32[2]{0:T(128)S(1)} all-reduce(f32[2]{0:T(128)S(1)} %get-tuple-element.119), channel_id=1, replica_groups=mesh['gx'=16,'gy'=4,'tx'=4] {'gx','gy'}, use_global_device_ids=true, to_apply=%region_5.7 | all-reduce | flops 2 | bytes 16 | tf_op jit(solution)/shard_map/psum | solution.py:135
  358.2 1.9 collective-permute-start
  360.2 5.8 collective-permute-start.1
  366.0 1.7 collective-permute-done.1
  368.5 1.9 collective-permute-start.2
  370.4 4.1 collective-permute-start.3
  374.6 4.7 collective-permute-done.2
  379.3 1.9 collective-permute-done.3
  381.2 2.4 select_maximum_fusion.12
  391.2 3.7 convolution_bitcast_fusion.7
  394.9 138.5 %all-gather.4 = f32[64,16,2]{1,2,0:T(2,128)S(1)} all-gather(f32[1,16,2]{1,2,0:T(2,128)S(1)} %convolution_bitcast_fusion.7), channel_id=2, replica_groups=mesh['gx'=16,'gy'=4,'tx'=4] {'gx','gy'}, dimensions={0}, use_global_device_ids=true | all-gather | bytes 8320 | tf_op jit(solution)/shard_map/all_gather | solution.py:141
  533.7 3.3 multiply_reduce_fusion.10
  537.0 139.0 %psum.87 = f32[1,2]{1,0:T(1,128)S(1)} all-reduce(f32[1,2]{1,0:T(1,128)S(1)} %bitcast.345), channel_id=1, replica_groups=mesh['gx'=16,'gy'=4,'tx'=4] {'gx','gy'}, use_global_device_ids=true, to_apply=%region_8.10 | all-reduce | flops 2 | bytes 16 | tf_op jit(solution)/shard_map/psum | solution.py:144
  676.7 140.2 %psum.88 = f32[2]{0:T(128)S(1)} all-reduce(f32[2]{0:T(128)S(1)} %get-tuple-element.49), channel_id=1, replica_groups=mesh['gx'=16,'gy'=4,'tx'=4] {'gx','gy'}, use_global_device_ids=true, to_apply=%region_10.12 | all-reduce | flops 2 | bytes 16 | tf_op jit(solution)/shard_map/psum | solution.py:147
  817.1 1.9 collective-permute-start.4
  819.0 5.8 collective-permute-start.5
  824.9 1.6 collective-permute-done.5
  827.3 1.9 collective-permute-start.6
  829.3 3.9 collective-permute-start.7
  833.3 4.9 collective-permute-done.6
  838.1 1.9 collective-permute-done.7
  840.1 2.4 select_maximum_fusion.8
  850.1 3.6 convolution_bitcast_fusion.6
  853.7 138.7 %all-gather.5 = f32[64,16,2]{1,2,0:T(2,128)S(1)} all-gather(f32[1,16,2]{1,2,0:T(2,128)S(1)} %convolution_bitcast_fusion.6), channel_id=3, replica_groups=mesh['gx'=16,'gy'=4,'tx'=4] {'gx','gy'}, dimensions={0}, use_global_device_ids=true | all-gather | bytes 8320 | tf_op jit(solution)/shard_map/all_gather | solution.py:141
  992.7 3.4 multiply_reduce_fusion.8
  996.2 139.0 %psum.89 = f32[2,2]{1,0:T(2,128)S(1)} all-reduce(f32[2,2]{1,0:T(2,128)S(1)} %pad_maximum_fusion.26), channel_id=1, replica_groups=mesh['gx'=16,'gy'=4,'tx'=4] {'gx','gy'}, use_global_device_ids=true, to_apply=%region_14.16 | all-reduce | flops 4 | bytes 32 | tf_op jit(solution)/shard_map/psum | solution.py:144
  1136.0 140.2 %psum.90 = f32[2]{0:T(128)S(1)} all-reduce(f32[2]{0:T(128)S(1)} %get-tuple-element.47), channel_id=1, replica_groups=mesh['gx'=16,'gy'=4,'tx'=4] {'gx','gy'}, use_global_device_ids=true, to_apply=%region_16.18 | all-reduce | flops 2 | bytes 16 | tf_op jit(solution)/shard_map/psum | solution.py:147
  1279.1 139.0 %psum.91 = f32[2]{0:T(128)S(1)} all-reduce(f32[2]{0:T(128)S(1)} %get-tuple-element.45), channel_id=1, replica_groups=mesh['gx'=16,'gy'=4,'tx'=4] {'gx','gy'}, use_global_device_ids=true, to_apply=%region_20.24 | all-reduce | flops 2 | bytes 16 | tf_op jit(solution)/shard_map/psum | solution.py:135
  1418.4 1.9 collective-permute-start.8
  1420.4 5.8 collective-permute-start.9
  1426.2 3.7 convolution_add_fusion
  1430.7 1.9 collective-permute-start.10
  1432.7 4.1 collective-permute-start.11
  1436.9 5.5 collective-permute-done.10
  1442.4 1.9 collective-permute-done.11
  1444.3 2.4 select_maximum_fusion.4
  1454.3 3.7 convolution_bitcast_fusion.5
  1458.0 138.3 %all-gather.6 = f32[64,16,2]{1,2,0:T(2,128)S(1)} all-gather(f32[1,16,2]{1,2,0:T(2,128)S(1)} %convolution_bitcast_fusion.5), channel_id=4, replica_groups=mesh['gx'=16,'gy'=4,'tx'=4] {'gx','gy'}, dimensions={0}, use_global_device_ids=true | all-gather | bytes 8320 | tf_op jit(solution)/shard_map/all_gather | solution.py:141
  1596.7 3.3 multiply_reduce_fusion.4
  1600.0 138.7 %psum.92 = f32[1,2]{1,0:T(1,128)S(1)} all-reduce(f32[1,2]{1,0:T(1,128)S(1)} %bitcast.346), channel_id=1, replica_groups=mesh['gx'=16,'gy'=4,'tx'=4] {'gx','gy'}, use_global_device_ids=true, to_apply=%region_23.27 | all-reduce | flops 2 | bytes 16 | tf_op jit(solution)/shard_map/psum | solution.py:144
  1739.3 140.5 %psum.93 = f32[2]{0:T(128)S(1)} all-reduce(f32[2]{0:T(128)S(1)} %get-tuple-element.43), channel_id=1, replica_groups=mesh['gx'=16,'gy'=4,'tx'=4] {'gx','gy'}, use_global_device_ids=true, to_apply=%region_25.29 | all-reduce | flops 2 | bytes 16 | tf_op jit(solution)/shard_map/psum | solution.py:147
  1880.0 1.9 collective-permute-start.12
  1882.0 5.8 collective-permute-start.13
  1887.9 1.6 collective-permute-done.13
  1890.3 1.9 collective-permute-start.14
  1892.2 3.9 collective-permute-start.15
  1896.2 4.9 collective-permute-done.14
  1901.1 1.9 collective-permute-done.15
  1903.0 2.4 select_maximum_fusion
  1913.0 3.7 convolution_bitcast_fusion.4
  1916.7 138.5 %all-gather.7 = f32[64,16,2]{1,2,0:T(2,128)S(1)} all-gather(f32[1,16,2]{1,2,0:T(2,128)S(1)} %convolution_bitcast_fusion.4), channel_id=5, replica_groups=mesh['gx'=16,'gy'=4,'tx'=4] {'gx','gy'}, dimensions={0}, use_global_device_ids=true | all-gather | bytes 8320 | tf_op jit(solution)/shard_map/all_gather | solution.py:141
  2055.6 3.4 multiply_reduce_fusion.2
  2059.0 139.0 %psum.94 = f32[2,2]{1,0:T(2,128)S(1)} all-reduce(f32[2,2]{1,0:T(2,128)S(1)} %pad_maximum_fusion.27), channel_id=1, replica_groups=mesh['gx'=16,'gy'=4,'tx'=4] {'gx','gy'}, use_global_device_ids=true, to_apply=%region_29.33 | all-reduce | flops 4 | bytes 32 | tf_op jit(solution)/shard_map/psum | solution.py:144
  2199.4 140.2 %psum.95 = f32[2]{0:T(128)S(1)} all-reduce(f32[2]{0:T(128)S(1)} %get-tuple-element.41), channel_id=1, replica_groups=mesh['gx'=16,'gy'=4,'tx'=4] {'gx','gy'}, use_global_device_ids=true, to_apply=%region_31.35 | all-reduce | flops 2 | bytes 16 | tf_op jit(solution)/shard_map/psum | solution.py:147
  2341.8 1.5 multiply_add_fusion
  2344.4 2.7 fusion
  2347.1 1.5 convolution_subtract_fusion
  (213 shorter events, 52.3 us)
Async XLA Ops:
  7.2 46.0 %all-gather.11.cloned.1.call-start = ((), (), s32[]{:S(2)}) async-start(), calls=%async_computation | async-start | bytes 1966080 | tf_op jit(solution)/shard_map/all_gather | solution.py:113
  7.9 1418.3 %all-gather.13.cloned.1.call-start = ((), (), s32[]{:S(2)}) async-start(), calls=%async_computation.1 | async-start | bytes 1966080 | tf_op jit(solution)/shard_map/all_gather | solution.py:112
  53.1 5.4 copy-start.1
  358.2 7.7 collective-permute-start
  360.2 7.5 collective-permute-start.1
  368.5 10.8 collective-permute-start.2
  370.4 10.8 collective-permute-start.3
  389.8 1.4 copy-start.2
  817.1 7.8 collective-permute-start.4
  819.0 7.5 collective-permute-start.5
  827.3 10.8 collective-permute-start.6
  829.3 10.8 collective-permute-start.7
  848.7 1.4 copy-start.3
  1418.4 11.5 collective-permute-start.8
  1420.4 9.5 collective-permute-start.9
  1430.7 11.7 collective-permute-start.10
  1432.7 11.7 collective-permute-start.11
  1452.9 1.4 copy-start.4
  1880.0 7.8 collective-permute-start.12
  1882.0 7.5 collective-permute-start.13
  1890.3 10.8 collective-permute-start.14
  1892.2 10.8 collective-permute-start.15
  1911.6 1.4 copy-start.5
  2340.4 4.0 copy-start
Sparse Core Ops, SparseCore 0:
  9.8 43.2 all-gather.10
  366.1 35.2 all-gather.12
